TPU v7x, 32 devices: a whole 2x2x4 slice. The times are simulated.
32 devices in a mesh: section: 2 (over x), dp: 4 (over z), mp: 4 (over y, core).
Axes of the slice: x: 2, y: 2, z: 4, core: 2. Of those that a mesh axis runs over, the one named last changes fastest.
Arguments:
- w_query: bfloat16 [2, 4096, 4096], P('section', None, 'mp'), may hold values from -0.09375 to 0.09375
- w_key: bfloat16 [2, 4096, 1024], P('section', None, 'mp'), may hold values from -0.09375 to 0.09375
- w_value: bfloat16 [2, 4096, 1024], P('section', None, 'mp'), may hold values from -0.09375 to 0.09375
- w_out: bfloat16 [2, 4096, 4096], P('section', 'mp'), may hold values from -0.09375 to 0.09375
- norm_gain: bfloat16 [2, 4096], P('section', 'mp'), may hold values from 0.099609375 to 1.8984375
- saved_input: bfloat16 [2, 2, 4, 64, 4096], P('section', None, 'dp', None, 'mp'), may hold values from -6 to 6
- saved_query: bfloat16 [2, 2, 4, 64, 4096], P('section', None, 'dp', None, 'mp'), may hold values from -5 to 5
- saved_key: bfloat16 [2, 2, 4, 64, 1024], P('section', None, 'dp', None, 'mp'), may hold values from -5 to 5
- saved_value: bfloat16 [2, 2, 4, 64, 1024], P('section', None, 'dp', None, 'mp'), may hold values from -6 to 6
- grad_in: bfloat16 [2, 4, 64, 4096], P('section', 'dp', None, 'mp'), may hold values from -0.29882812 to 0.29882812
- fresh_grad: bfloat16 [1, 4, 64, 4096], P(None, 'dp', None, 'mp'), may hold values from -0.29882812 to 0.29882812
- features: bfloat16 [2, 4, 16, 7680], P(None, 'dp', None, 'section'), may hold values from -6 to 6
- image_pos: int32 [2, 4, 16], P(None, 'dp'), may hold values from 0 to 63, as said below
Outputs:
- proj_grad: bfloat16 [7680, 4096], P(('section', 'dp'), 'mp')
- pending: bfloat16 [2, 4, 64, 4096], P('section', 'dp', None, 'mp')
Inputs may be any that keep to these rules, and one draw needn't show every extreme that they name: `image_pos`: each row holds 16 consecutive ascending positions; the first row starts at 0 and the last ends at 63.
All inputs are finite; a program needn't handle non-finite values.
Results may differ from a plain program's by a relative error of at most 0.017.
Values may be sent and summed in bfloat16 or wider, within the bound.
A program may use at most 64 MiB of HBM per device.

v0:
```python
import jax
import jax.numpy as jnp
from jax import lax
from jax.sharding import PartitionSpec as P

D = 4096
HD = 128
TICKS = 2


def shifted(block, axis, distance):
    devices = range(lax.axis_size(axis))
    route = [(i - distance, i) for i in devices if i - distance in devices]
    return lax.ppermute(block, axis, route)


def spread_2(block, axis, holder):
    block = jnp.where(lax.axis_index(axis) == holder, block, jnp.zeros_like(block))
    return lax.psum(block, axis)


def attention_back(query, key_in, value, d_attn):
    seq_len = query.shape[0]
    kv_local = key_in.shape[1] // HD
    group = query.shape[1] // key_in.shape[1]
    scale = HD ** (-0.5)
    q_four = query.reshape(seq_len, kv_local, group, HD)
    k_three = key_in.reshape(seq_len, kv_local, HD)
    v_three = value.reshape(seq_len, kv_local, HD)
    a_four = d_attn.reshape(seq_len, kv_local, group, HD)
    scores = (
        jnp.einsum("lgjd,mgd->gjlm", q_four, k_three, preferred_element_type=jnp.float32) * scale
    )
    rows = jnp.arange(seq_len)[:, None]
    cols = jnp.arange(seq_len)[None, :]
    scores = jnp.where(cols <= rows, scores, -1e30)
    top = jnp.max(scores, -1, keepdims=True)
    expo = jnp.exp(scores - top)
    probs = expo / jnp.sum(expo, -1, keepdims=True)
    d_probs = jnp.einsum("lgjd,mgd->gjlm", a_four, v_three, preferred_element_type=jnp.float32)
    inner = jnp.sum(probs * d_probs, -1, keepdims=True)
    d_scores = (probs * (d_probs - inner) * scale).astype(jnp.bfloat16)
    probs_half = probs.astype(jnp.bfloat16)
    d_query = jnp.einsum(
        "gjlm,mgd->lgjd", d_scores, k_three, preferred_element_type=jnp.float32
    ).astype(jnp.bfloat16)
    d_key = jnp.einsum(
        "gjlm,lgjd->mgd", d_scores, q_four, preferred_element_type=jnp.float32
    ).astype(jnp.bfloat16)
    d_value = jnp.einsum(
        "gjlm,lgjd->mgd", probs_half, a_four, preferred_element_type=jnp.float32
    ).astype(jnp.bfloat16)
    return (d_query.reshape(seq_len, -1), d_key.reshape(seq_len, -1), d_value.reshape(seq_len, -1))


def segment_step(grad, x_saved, gain, w_q, w_k, w_v, w_o, query, key_in, value):
    x_float = x_saved.astype(jnp.float32)
    squares_local = jnp.sum(x_float * x_float, -1)
    d_attn = lax.dot_general(
        lax.all_gather(grad, "mp", axis=1, tiled=True),
        w_o,
        (((1,), (1,)), ((), ())),
        preferred_element_type=jnp.float32,
    ).astype(jnp.bfloat16)
    d_query, d_key, d_value = attention_back(query, key_in, value, d_attn)
    contract = (((1,), (1,)), ((), ()))
    partial_term = lax.dot_general(d_query, w_q, contract, preferred_element_type=jnp.float32)
    partial_term = partial_term + lax.dot_general(
        d_key, w_k, contract, preferred_element_type=jnp.float32
    )
    partial_term = partial_term + lax.dot_general(
        d_value, w_v, contract, preferred_element_type=jnp.float32
    )
    d_normed = lax.psum_scatter(
        partial_term.astype(jnp.bfloat16), "mp", scatter_dimension=1, tiled=True
    ).astype(jnp.float32)
    weighted = gain.astype(jnp.float32) * d_normed
    cross_local = jnp.sum(x_float * weighted, -1)
    squares, cross = lax.psum((squares_local, cross_local), "mp")
    rstd = lax.rsqrt(squares / D + 1e-05)[:, None]
    d_input = rstd * weighted - x_float * rstd**3 * (cross / D)[:, None]
    return (grad.astype(jnp.float32) + d_input).astype(jnp.bfloat16)


def shards(
    w_query,
    w_key,
    w_value,
    w_out,
    norm_gain,
    saved_input,
    saved_query,
    saved_key,
    saved_value,
    grad_in,
    fresh_grad,
    features,
    image_pos,
):
    segments = lax.axis_size("section")
    here = lax.axis_index("section")
    held = grad_in[0, 0]
    picks = []
    produced = held
    for tick in range(TICKS):
        produced = segment_step(
            held,
            saved_input[0, tick, 0],
            norm_gain[0],
            w_query[0],
            w_key[0],
            w_value[0],
            w_out[0],
            saved_query[0, tick, 0],
            saved_key[0, tick, 0],
            saved_value[0, tick, 0],
        )
        picks.append(jnp.take(produced, image_pos[tick, 0], axis=0))
        if tick + 1 < TICKS:
            moved = shifted(produced, "section", -1)
            held = jnp.where(here == segments - 1, fresh_grad[tick, 0], moved)
    image_grad = spread_2(jnp.stack(picks), "section", 0)
    spread = lax.all_to_all(features, "dp", split_axis=3, concat_axis=1, tiled=True)
    total = jnp.einsum(
        "knif,knid->fd",
        spread,
        lax.all_gather(image_grad[:, None], "dp", axis=1, tiled=True),
        preferred_element_type=jnp.float32,
    )
    return (total.astype(jnp.bfloat16), produced[None, None])


def solution(mesh):
    in_specs = (
        P("section", None, "mp"),
        P("section", None, "mp"),
        P("section", None, "mp"),
        P("section", "mp", None),
        P("section", "mp"),
        P("section", None, "dp", None, "mp"),
        P("section", None, "dp", None, "mp"),
        P("section", None, "dp", None, "mp"),
        P("section", None, "dp", None, "mp"),
        P("section", "dp", None, "mp"),
        P(None, "dp", None, "mp"),
        P(None, "dp", None, "section"),
        P(None, "dp", None),
    )
    out_specs = (P(("section", "dp"), "mp"), P("section", "dp", None, "mp"))
    return jax.shard_map(shards, mesh=mesh, in_specs=in_specs, out_specs=out_specs, check_vma=False)
```

profile of v0, /device:TPU:0, one launch (start us, length us, event | category | flops | bytes accessed | tf_op | source)
XLA Modules:
  0.0 174.8 jit_solution(17616110696914920149)
XLA Ops:
  10.1 8.9 %all-gather = bf16[1,1,64,4096]{3,2,1,0:T(8,128)(2,1)S(1)} all-gather(bf16[1,1,64,1024]{3,2,1,0:T(8,128)(2,1)} %param.24), channel_id=2, replica_groups=mesh['section'=2,'dp'=4,'mp'=4] {'mp'}, dimensions={3}, use_global_device_ids=true | all-gather | bytes 655360 | tf_op jit(solution)/shard_map/all_gather | solution.py:60
  18.9 6.0 %fusion.35 = bf16[64,1024]{1,0:T(8,128)(2,1)S(1)} fusion(bf16[1,1024,4096]{2,1,0:T(8,128)(2,1)} %param.18, bf16[1,1,64,4096]{3,2,1,0:T(8,128)(2,1)S(1)} %all-gather), kind=kOutput, calls=%fused_computation.46 | convolution fusion | flops 536936448 | bytes 9043968 | tf_op jit(solution)/shard_map/dot_general | solution.py:59
  26.6 6.0 %fusion.6 = f32[64,4096]{1,0:T(8,128)S(1)} fusion(bf16[64,1024]{1,0:T(8,128)(2,1)S(1)} %reshape.54, bf16[1,4096,1024]{2,1,0:T(8,128)(2,1)} %param.15), kind=kOutput, calls=%fused_computation.8 | convolution fusion | flops 536870912 | bytes 9568256 | tf_op jit(solution)/shard_map/dot_general | solution.py:67
  34.2 1.6 fusion.12
  36.0 22.4 %reduce-scatter.3.cloned.1.call-done = bf16[64,1024]{1,0:T(8,128)(2,1)} async-done(((bf16[64,4096]{1,0:T(8,128)(2,1)}), bf16[64,1024]{1,0:T(8,128)(2,1)}) %reduce-scatter.3.cloned.1.call-update) | async-done | bytes 131088 | tf_op jit(solution)/shard_map/reduce_scatter | solution.py:74
  59.5 5.8 %all-reduce.1 = (f32[64]{0:T(128)S(1)}, f32[64]{0:T(128)S(1)}) all-reduce(f32[64]{0:T(128)S(1)} %get-tuple-element.4, f32[64]{0:T(128)S(1)} %get-tuple-element.5), channel_id=1, replica_groups=mesh['section'=2,'dp'=4,'mp'=4] {'mp'}, use_global_device_ids=true, to_apply=%region_7.8 | all-reduce | flops 128 | bytes 1024 | tf_op jit(solution)/shard_map/psum | solution.py:79
  66.4 1.3 collective-permute-start
  68.7 4.8 %collective-permute-done = bf16[64,1024]{1,0:T(8,128)(2,1)S(1)} collective-permute-done((bf16[64,1024]{1,0:T(8,128)(2,1)S(1)}, bf16[64,1024]{1,0:T(8,128)(2,1)S(1)}, u32[]{:S(2)}, u32[]{:S(2)}) %collective-permute-start) | collective-permute-done | bytes 131104 | tf_op jit(solution)/shard_map/ppermute | solution.py:14
  73.5 6.9 %all_gather.10 = bf16[64,4096]{1,0:T(8,128)(2,1)S(1)} all-gather(bf16[64,1024]{1,0:T(8,128)(2,1)S(1)} %bitcast_select_fusion), channel_id=1, replica_groups=mesh['section'=2,'dp'=4,'mp'=4] {'mp'}, dimensions={1}, use_global_device_ids=true | all-gather | bytes 655360 | tf_op jit(solution)/shard_map/all_gather | solution.py:60
  80.3 6.0 %fusion.38 = bf16[64,1024]{1,0:T(8,128)(2,1)S(1)} fusion(bf16[64,4096]{1,0:T(8,128)(2,1)S(1)} %all_gather.10, bf16[1,1024,4096]{2,1,0:T(8,128)(2,1)} %param.18), kind=kOutput, calls=%fused_computation.47 | convolution fusion | flops 536936448 | bytes 9043968 | tf_op jit(solution)/shard_map/dot_general | solution.py:59
  87.9 1.3 fusion.49
  89.2 1.3 fusion.42
  90.7 6.0 %fusion.4 = f32[64,4096]{1,0:T(8,128)S(1)} fusion(bf16[64,1024]{1,0:T(8,128)(2,1)S(1)} %reshape.58, bf16[1,4096,1024]{2,1,0:T(8,128)(2,1)} %param.15), kind=kOutput, calls=%fused_computation.6 | convolution fusion | flops 536870912 | bytes 9568256 | tf_op jit(solution)/shard_map/dot_general | solution.py:67
  98.3 1.6 fusion.13
  99.9 3.1 %copy.91 = bf16[2,1,16,3840]{2,0,1,3:T(2,128)(2,1)} copy(bf16[2,1,16,3840]{3,2,1,0:T(8,128)(2,1)S(1)} %copy-done.6) | data formatting | bytes 491520 | tf_op args[11]
  103.0 3.9 %reshape.99 = bf16[4,2,15360]{2,1,0:T(2,128)(2,1)} reshape(bf16[3840,1,2,16]{3,2,1,0:T(2,128)(2,1)} %bitcast.175) | data formatting | bytes 491520
  106.9 4.6 %all-to-all-start = ((bf16[4,2,15360]{2,1,0:T(2,128)(2,1)}), bf16[4,2,15360]{2,1,0:T(2,128)(2,1)S(1)}, u32[]{:S(2)}, u32[]{:S(2)}) async-start(bf16[4,2,15360]{2,1,0:T(2,128)(2,1)} %reshape.99), calls=%async_computation.2 | async-start | bytes 491520 | tf_op jit(solution)/shard_map/all_to_all | solution.py:123
  112.2 9.1 %reduce-scatter.5.cloned.1.call-done = bf16[64,1024]{1,0:T(8,128)(2,1)} async-done(((bf16[64,4096]{1,0:T(8,128)(2,1)}), bf16[64,1024]{1,0:T(8,128)(2,1)}) %reduce-scatter.5.cloned.1.call-update) | async-done | bytes 131088 | tf_op jit(solution)/shard_map/reduce_scatter | solution.py:74
  122.3 5.8 %all-reduce = (f32[64]{0:T(128)S(1)}, f32[64]{0:T(128)S(1)}) all-reduce(f32[64]{0:T(128)S(1)} %fusion.71, f32[64]{0:T(128)S(1)} %get-tuple-element.3), channel_id=1, replica_groups=mesh['section'=2,'dp'=4,'mp'=4] {'mp'}, use_global_device_ids=true, to_apply=%region_15.17 | all-reduce | flops 128 | bytes 1024 | tf_op jit(solution)/shard_map/psum | solution.py:79
  130.5 2.3 %reshape.100 = bf16[3840,1,2,16]{3,2,1,0:T(2,128)(2,1)} reshape(bf16[4,2,15360]{2,1,0:T(2,128)(2,1)S(1)} %all-to-all-done) | data formatting | bytes 491520
  132.8 4.5 %copy.93 = bf16[2,1,16,4,960]{4,2,3,0,1:T(8,128)(2,1)S(1)} copy(bf16[2,1,16,4,960]{2,0,4,3,1:T(2,128)(2,1)} %bitcast.174) | data formatting | bytes 491520 | tf_op jit(solution)/shard_map/all_to_all | solution.py:123
  137.3 14.9 %all-reduce.4.cloned.1.call-done = bf16[2,1,16,1024]{3,2,1,0:T(8,128)(2,1)} async-done(((bf16[2,1,16,1024]{3,2,1,0:T(8,128)(2,1)}), bf16[2,1,16,1024]{3,2,1,0:T(8,128)(2,1)}) %all-reduce.4.cloned.1.call-update) | async-done | bytes 65552 | tf_op jit(solution)/shard_map/psum | solution.py:19
  152.2 14.1 %all_gather.11 = bf16[2,4,16,1024]{3,2,1,0:T(8,128)(2,1)S(1)} all-gather(bf16[2,1,16,1024]{3,2,1,0:T(8,128)(2,1)} %all-reduce.4.cloned.1.call-done), channel_id=1, replica_groups=mesh['section'=2,'dp'=4,'mp'=4] {'dp'}, dimensions={1}, use_global_device_ids=true | all-gather | bytes 327680 | tf_op jit(solution)/shard_map/all_gather | solution.py:127
  166.3 2.0 %fusion.18 = bf16[960,1024]{1,0:T(8,128)(2,1)} fusion(bf16[2,4,16,1024]{3,2,1,0:T(8,128)(2,1)S(1)} %all_gather.11, bf16[2,1,16,4,960]{4,2,3,0,1:T(8,128)(2,1)S(1)} %copy.93), kind=kOutput, calls=%fused_computation.25 | convolution fusion | flops 252641280 | bytes 2473984 | tf_op jit(solution)/shard_map/knif,knid->fd/dot_general | solution.py:124
  (70 shorter events, 16.8 us)
Async XLA Ops:
  7.2 25.4 %copy-start = (bf16[1,4096,256]{2,1,0:T(8,128)(2,1)S(1)}, bf16[1,4096,256]{2,1,0:T(8,128)(2,1)}, u32[]{:S(2)}) copy-start(bf16[1,4096,256]{2,1,0:T(8,128)(2,1)} %param.16) | copy-start | bytes 6291460
  7.2 51.2 %reduce-scatter.3.cloned.1.call-start = ((), (), s32[]{:S(2)}) async-start(), calls=%async_computation.3 | async-start | bytes 655360 | tf_op jit(solution)/shard_map/reduce_scatter | solution.py:74
  32.6 1.6 copy-start.1
  34.2 1.6 copy-start.8
  34.2 24.2 %copy-start.3 = (bf16[1,2,1,64,1024]{4,3,2,1,0:T(8,128)(2,1)S(1)}, bf16[1,2,1,64,1024]{4,3,2,1,0:T(8,128)(2,1)}, u32[]{:S(2)}) copy-start(bf16[1,2,1,64,1024]{4,3,2,1,0:T(8,128)(2,1)} %param.20) | copy-start | bytes 786436
  34.2 31.1 %copy-start.5 = (bf16[1,1,64,1024]{3,2,1,0:T(8,128)(2,1)S(1)}, bf16[1,1,64,1024]{3,2,1,0:T(8,128)(2,1)}, u32[]{:S(2)}) copy-start(bf16[1,1,64,1024]{3,2,1,0:T(8,128)(2,1)} %param.24) | copy-start | bytes 393220
  35.8 37.7 %copy-start.7 = (bf16[1,1,64,1024]{3,2,1,0:T(8,128)(2,1)S(1)}, bf16[1,1,64,1024]{3,2,1,0:T(8,128)(2,1)}, u32[]{:S(2)}) copy-start(bf16[1,1,64,1024]{3,2,1,0:T(8,128)(2,1)} %param.25) | copy-start | bytes 393220
  35.8 85.4 %reduce-scatter.5.cloned.1.call-start = ((), (), s32[]{:S(2)}) async-start(), calls=%async_computation.4 | async-start | bytes 655360 | tf_op jit(solution)/shard_map/reduce_scatter | solution.py:74
  66.4 7.1 %collective-permute-start = (bf16[64,1024]{1,0:T(8,128)(2,1)S(1)}, bf16[64,1024]{1,0:T(8,128)(2,1)S(1)}, u32[]{:S(2)}, u32[]{:S(2)}) collective-permute-start(bf16[64,1024]{1,0:T(8,128)(2,1)S(1)} %fusion.64), channel_id=1, source_target_pairs={{16,0},{17,1},{18,2},{19,3},{20,4},{21,5},{22,6},{23,7},{24,8},{25... | collective-permute-start | bytes 393224 | tf_op jit(solution)/shard_map/ppermute | solution.py:14
  96.7 1.6 copy-start.2
  98.3 1.6 copy-start.6
  99.9 11.6 %copy-start.9 = (s32[2,1,16]{2,1,0:T(1,128)S(1)}, s32[2,1,16]{2,1,0:T(1,128)}, u32[]{:S(2)}) copy-start(s32[2,1,16]{2,1,0:T(1,128)} %param.27) | copy-start | bytes 388
  106.9 23.6 %all-to-all-start = ((bf16[4,2,15360]{2,1,0:T(2,128)(2,1)}), bf16[4,2,15360]{2,1,0:T(2,128)(2,1)S(1)}, u32[]{:S(2)}, u32[]{:S(2)}) async-start(bf16[4,2,15360]{2,1,0:T(2,128)(2,1)} %reshape.99), calls=%async_computation.2 | async-start | bytes 491520 | tf_op jit(solution)/shard_map/all_to_all | solution.py:123
  111.5 40.7 %all-reduce.4.cloned.1.call-start = ((), (), s32[]{:S(2)}) async-start(), calls=%async_computation.5 | async-start | bytes 131072 | tf_op jit(solution)/shard_map/psum | solution.py:19
  129.1 8.1 %copy-start.4 = (bf16[64,1024]{1,0:T(8,128)(2,1)}, bf16[64,1024]{1,0:T(8,128)(2,1)S(1)}, u32[]{:S(2)}) copy-start(bf16[64,1024]{1,0:T(8,128)(2,1)S(1)} %fusion.70) | copy-start | bytes 393220
Sparse Core Ops, SparseCore 0:
  35.9 22.4 reduce-scatter.2
  100.0 21.1 reduce-scatter.4
  130.6 21.5 all-reduce.3
where the time goes:
time: 176 us; the launch traced here: 175 us
  waiting for transfers between devices  51.2 us (29%)
  blocking collectives  41.4 us (24%)
  matrix products  37.1 us (21%)
  local copies, waits for them, and re-layouts  20 us (11%)
  between operations  14 us (8%)
  starting transfers between devices  5.97 us (3%)
  other arithmetic  5.13 us (3%)
    reduce_scatter x2, waiting for transfers between devices, segment_step(): lax.psum_scatter(partial_term.astype(jnp.bfloat16), 'mp', scatter_dimensi...  31.5 us
    all_gather x2, blocking collectives, segment_step(): lax.all_gather(grad, 'mp', axis=1, tiled=True)  15.8 us
    psum x1, waiting for transfers between devices, spread_2(): return lax.psum(block, axis)  14.9 us
    all_gather x1, blocking collectives, shards(): lax.all_gather(image_grad[:, None], 'dp', axis=1, tiled=True)  14.1 us
    dot_general x2, matrix products, segment_step(): lax.dot_general(lax.all_gather(grad, 'mp', axis=1, tiled=True), w_o, (((1...  12.1 us
    dot_general x2, matrix products, segment_step(): lax.dot_general(d_query, w_q, contract, preferred_element_type=jnp.float32)  12.1 us
    psum x2, blocking collectives, segment_step(): squares, cross = lax.psum((squares_local, cross_local), 'mp')  11.5 us
    unnamed x23, local copies, waits for them, and re-layouts  10.9 us
  transfers between devices with their start and end apart: 5, of which 4 were waited for; matrix products, arithmetic and copies ran while one was open for 11% of the time, Pallas kernels for 0%

commit v1 on v0

--- a/solution.py
+++ b/solution.py
@@ -16,7 +16,7 @@
 
 def spread_2(block, axis, holder):
     block = jnp.where(lax.axis_index(axis) == holder, block, jnp.zeros_like(block))
-    return lax.psum(block, axis)
+    return jnp.sum(lax.all_gather(block, axis), axis=0)
 
 
 def attention_back(query, key_in, value, d_attn):

time: 176 us -> 165 us (0.938)
  waiting for transfers between devices: 51.2 us -> 36.2 us
  blocking collectives: 41.4 us -> 46.5 us
    psum x1 -> x0, waiting for transfers between devices: 14.9 us -> none  [spread_2(): return lax.psum(block, axis)]
    reduce_scatter x2, waiting for transfers between devices: 31.5 us -> 22.4 us  [segment_step(): lax.psum_scatter(partial_term.astype(jnp.bfloat16), 'mp', scatter_dimensi...]
    all_to_all x1, waiting for transfers between devices: 0.01 us -> 9 us  [shards(): lax.all_to_all(features, 'dp', split_axis=3, concat_axis=1, tiled=True)]
    all_gather x0 -> x1, blocking collectives: none -> 4.93 us  [spread_2(): return jnp.sum(lax.all_gather(block, axis), axis=0)]
  transfers between devices with their start and end apart: 5 -> 4, of which waited for: 4 -> 3; matrix products, arithmetic and copies ran while one was open for 11% -> 9% of each run, Pallas kernels for 0% -> 0%
where the time goes in v1:
time: 165 us
  blocking collectives  46.5 us (28%)
  matrix products  37.1 us (22%)
  waiting for transfers between devices  36.2 us (22%)
  local copies, waits for them, and re-layouts  20 us (12%)
  between operations  14.3 us (9%)
  starting transfers between devices  5.97 us (4%)
  other arithmetic  4.53 us (3%)
    reduce_scatter x2, waiting for transfers between devices, segment_step(): lax.psum_scatter(partial_term.astype(jnp.bfloat16), 'mp', scatter_dimensi...  22.4 us
    all_gather x2, blocking collectives, segment_step(): lax.all_gather(grad, 'mp', axis=1, tiled=True)  15.8 us
    all_gather x1, blocking collectives, shards(): lax.all_gather(image_grad[:, None], 'dp', axis=1, tiled=True)  14.4 us
    dot_general x2, matrix products, segment_step(): lax.dot_general(lax.all_gather(grad, 'mp', axis=1, tiled=True), w_o, (((1...  12.1 us
    dot_general x2, matrix products, segment_step(): lax.dot_general(d_query, w_q, contract, preferred_element_type=jnp.float32)  12.1 us
    psum x2, blocking collectives, segment_step(): squares, cross = lax.psum((squares_local, cross_local), 'mp')  11.4 us
    unnamed x23, local copies, waits for them, and re-layouts  10.9 us
    all_to_all x1, waiting for transfers between devices, shards(): lax.all_to_all(features, 'dp', split_axis=3, concat_axis=1, tiled=True)  9 us
  transfers between devices with their start and end apart: 4, of which 3 were waited for; matrix products, arithmetic and copies ran while one was open for 9% of the time, Pallas kernels for 0%

profile of v1, /device:TPU:0, one launch (start us, length us, event | category | flops | bytes accessed | tf_op | source)
XLA Modules:
  0.0 164.6 jit_solution(8561839415696745284)
XLA Ops:
  10.1 8.9 %all-gather = bf16[1,1,64,4096]{3,2,1,0:T(8,128)(2,1)S(1)} all-gather(bf16[1,1,64,1024]{3,2,1,0:T(8,128)(2,1)} %param.24), channel_id=2, replica_groups=mesh['section'=2,'dp'=4,'mp'=4] {'mp'}, dimensions={3}, use_global_device_ids=true | all-gather | bytes 655360 | tf_op jit(solution)/shard_map/all_gather | solution.py:60
  18.9 6.0 %fusion.35 = bf16[64,1024]{1,0:T(8,128)(2,1)S(1)} fusion(bf16[1,1024,4096]{2,1,0:T(8,128)(2,1)} %param.18, bf16[1,1,64,4096]{3,2,1,0:T(8,128)(2,1)S(1)} %all-gather), kind=kOutput, calls=%fused_computation.46 | convolution fusion | flops 536936448 | bytes 9043968 | tf_op jit(solution)/shard_map/dot_general | solution.py:59
  26.6 6.0 %fusion.6 = f32[64,4096]{1,0:T(8,128)S(1)} fusion(bf16[64,1024]{1,0:T(8,128)(2,1)S(1)} %reshape.85, bf16[1,4096,1024]{2,1,0:T(8,128)(2,1)} %param.15), kind=kOutput, calls=%fused_computation.8 | convolution fusion | flops 536870912 | bytes 9568256 | tf_op jit(solution)/shard_map/dot_general | solution.py:67
  34.2 1.6 fusion.12
  36.0 22.4 %reduce-scatter.3.cloned.1.call-done = bf16[64,1024]{1,0:T(8,128)(2,1)} async-done(((bf16[64,4096]{1,0:T(8,128)(2,1)}), bf16[64,1024]{1,0:T(8,128)(2,1)}) %reduce-scatter.3.cloned.1.call-update) | async-done | bytes 131088 | tf_op jit(solution)/shard_map/reduce_scatter | solution.py:74
  59.5 5.8 %all-reduce.1 = (f32[64]{0:T(128)S(1)}, f32[64]{0:T(128)S(1)}) all-reduce(f32[64]{0:T(128)S(1)} %get-tuple-element.4, f32[64]{0:T(128)S(1)} %get-tuple-element.5), channel_id=1, replica_groups=mesh['section'=2,'dp'=4,'mp'=4] {'mp'}, use_global_device_ids=true, to_apply=%region_7.8 | all-reduce | flops 128 | bytes 1024 | tf_op jit(solution)/shard_map/psum | solution.py:79
  66.4 1.3 collective-permute-start
  68.7 4.8 %collective-permute-done = bf16[64,1024]{1,0:T(8,128)(2,1)S(1)} collective-permute-done((bf16[64,1024]{1,0:T(8,128)(2,1)S(1)}, bf16[64,1024]{1,0:T(8,128)(2,1)S(1)}, u32[]{:S(2)}, u32[]{:S(2)}) %collective-permute-start) | collective-permute-done | bytes 131104 | tf_op jit(solution)/shard_map/ppermute | solution.py:14
  73.5 6.9 %all_gather.14 = bf16[64,4096]{1,0:T(8,128)(2,1)S(1)} all-gather(bf16[64,1024]{1,0:T(8,128)(2,1)S(1)} %bitcast_select_fusion), channel_id=1, replica_groups=mesh['section'=2,'dp'=4,'mp'=4] {'mp'}, dimensions={1}, use_global_device_ids=true | all-gather | bytes 655360 | tf_op jit(solution)/shard_map/all_gather | solution.py:60
  80.3 6.0 %fusion.38 = bf16[64,1024]{1,0:T(8,128)(2,1)S(1)} fusion(bf16[64,4096]{1,0:T(8,128)(2,1)S(1)} %all_gather.14, bf16[1,1024,4096]{2,1,0:T(8,128)(2,1)} %param.18), kind=kOutput, calls=%fused_computation.47 | convolution fusion | flops 536936448 | bytes 9043968 | tf_op jit(solution)/shard_map/dot_general | solution.py:59
  87.9 1.3 fusion.49
  89.2 1.3 fusion.42
  90.7 6.0 %fusion.4 = f32[64,4096]{1,0:T(8,128)S(1)} fusion(bf16[64,1024]{1,0:T(8,128)(2,1)S(1)} %reshape.89, bf16[1,4096,1024]{2,1,0:T(8,128)(2,1)} %param.15), kind=kOutput, calls=%fused_computation.6 | convolution fusion | flops 536870912 | bytes 9568256 | tf_op jit(solution)/shard_map/dot_general | solution.py:67
  98.3 1.6 fusion.13
  99.9 3.1 %copy.91 = bf16[2,1,16,3840]{2,0,1,3:T(2,128)(2,1)} copy(bf16[2,1,16,3840]{3,2,1,0:T(8,128)(2,1)S(1)} %copy-done.6) | data formatting | bytes 491520 | tf_op args[11]
  103.0 3.9 %reshape.131 = bf16[4,2,15360]{2,1,0:T(2,128)(2,1)} reshape(bf16[3840,1,2,16]{3,2,1,0:T(2,128)(2,1)} %bitcast.174) | data formatting | bytes 491520
  106.9 4.6 %all-to-all-start = ((bf16[4,2,15360]{2,1,0:T(2,128)(2,1)}), bf16[4,2,15360]{2,1,0:T(2,128)(2,1)S(1)}, u32[]{:S(2)}, u32[]{:S(2)}) async-start(bf16[4,2,15360]{2,1,0:T(2,128)(2,1)} %reshape.131), calls=%async_computation.2 | async-start | bytes 491520 | tf_op jit(solution)/shard_map/all_to_all | solution.py:123
  111.5 9.0 %all-to-all-done = bf16[4,2,15360]{2,1,0:T(2,128)(2,1)S(1)} async-done(((bf16[4,2,15360]{2,1,0:T(2,128)(2,1)}), bf16[4,2,15360]{2,1,0:T(2,128)(2,1)S(1)}, u32[]{:S(2)}, u32[]{:S(2)}) %all-to-all-start) | async-done | bytes 245792 | tf_op jit(solution)/shard_map/all_to_all | solution.py:123
  120.5 2.3 %reshape.132 = bf16[3840,1,2,16]{3,2,1,0:T(2,128)(2,1)} reshape(bf16[4,2,15360]{2,1,0:T(2,128)(2,1)S(1)} %all-to-all-done) | data formatting | bytes 491520
  122.8 4.5 %copy.93 = bf16[2,1,16,4,960]{4,2,3,0,1:T(8,128)(2,1)S(1)} copy(bf16[2,1,16,4,960]{2,0,4,3,1:T(2,128)(2,1)} %bitcast.173) | data formatting | bytes 491520 | tf_op jit(solution)/shard_map/all_to_all | solution.py:123
  129.0 5.7 %all-reduce = (f32[64]{0:T(128)S(1)}, f32[64]{0:T(128)S(1)}) all-reduce(f32[64]{0:T(128)S(1)} %fusion.71, f32[64]{0:T(128)S(1)} %get-tuple-element.3), channel_id=1, replica_groups=mesh['section'=2,'dp'=4,'mp'=4] {'mp'}, use_global_device_ids=true, to_apply=%region_15.17 | all-reduce | flops 128 | bytes 1024 | tf_op jit(solution)/shard_map/psum | solution.py:79
  136.4 4.9 %all_gather.15 = bf16[2,2,16,1024]{3,2,1,0:T(8,128)(2,1)S(1)} all-gather(bf16[1,2,16,1024]{3,2,1,0:T(8,128)(2,1)S(1)} %maximum_select_fusion), channel_id=1, replica_groups=mesh['section'=2,'dp'=4,'mp'=4] {'section'}, dimensions={0}, use_global_device_ids=true | all-gather | bytes 196608 | tf_op jit(solution)/shard_map/all_gather | solution.py:19
  141.4 14.4 %all-gather.1 = bf16[2,64,1024]{2,1,0:T(8,128)(2,1)S(1)} all-gather(bf16[2,16,1024]{2,1,0:T(8,128)(2,1)S(1)} %reduce_sum.92), channel_id=3, replica_groups=mesh['section'=2,'dp'=4,'mp'=4] {'dp'}, dimensions={1}, use_global_device_ids=true | all-gather | bytes 327680 | tf_op jit(solution)/shard_map/all_gather | solution.py:127
  155.7 2.0 %fusion.18 = bf16[960,1024]{1,0:T(8,128)(2,1)} fusion(bf16[2,4,16,1024]{3,2,1,0:T(8,128)(2,1)S(1)} %bitcast.176, bf16[2,1,16,4,960]{4,2,3,0,1:T(8,128)(2,1)S(1)} %copy.93), kind=kOutput, calls=%fused_computation.25 | convolution fusion | flops 252641280 | bytes 2473984 | tf_op jit(solution)/shard_map/knif,knid->fd/dot_general | solution.py:124
  (69 shorter events, 16.1 us)
Async XLA Ops:
  7.2 25.4 %copy-start = (bf16[1,4096,256]{2,1,0:T(8,128)(2,1)S(1)}, bf16[1,4096,256]{2,1,0:T(8,128)(2,1)}, u32[]{:S(2)}) copy-start(bf16[1,4096,256]{2,1,0:T(8,128)(2,1)} %param.16) | copy-start | bytes 6291460
  7.2 51.2 %reduce-scatter.3.cloned.1.call-start = ((), (), s32[]{:S(2)}) async-start(), calls=%async_computation.3 | async-start | bytes 655360 | tf_op jit(solution)/shard_map/reduce_scatter | solution.py:74
  32.6 1.6 copy-start.1
  34.2 1.6 copy-start.8
  34.2 24.2 %copy-start.3 = (bf16[1,2,1,64,1024]{4,3,2,1,0:T(8,128)(2,1)S(1)}, bf16[1,2,1,64,1024]{4,3,2,1,0:T(8,128)(2,1)}, u32[]{:S(2)}) copy-start(bf16[1,2,1,64,1024]{4,3,2,1,0:T(8,128)(2,1)} %param.20) | copy-start | bytes 786436
  34.2 31.1 %copy-start.5 = (bf16[1,1,64,1024]{3,2,1,0:T(8,128)(2,1)S(1)}, bf16[1,1,64,1024]{3,2,1,0:T(8,128)(2,1)}, u32[]{:S(2)}) copy-start(bf16[1,1,64,1024]{3,2,1,0:T(8,128)(2,1)} %param.24) | copy-start | bytes 393220
  35.8 37.7 %copy-start.7 = (bf16[1,1,64,1024]{3,2,1,0:T(8,128)(2,1)S(1)}, bf16[1,1,64,1024]{3,2,1,0:T(8,128)(2,1)}, u32[]{:S(2)}) copy-start(bf16[1,1,64,1024]{3,2,1,0:T(8,128)(2,1)} %param.25) | copy-start | bytes 393220
  35.8 92.1 %reduce-scatter.5.cloned.1.call-start = ((), (), s32[]{:S(2)}) async-start(), calls=%async_computation.4 | async-start | bytes 655360 | tf_op jit(solution)/shard_map/reduce_scatter | solution.py:74
  66.4 7.1 %collective-permute-start = (bf16[64,1024]{1,0:T(8,128)(2,1)S(1)}, bf16[64,1024]{1,0:T(8,128)(2,1)S(1)}, u32[]{:S(2)}, u32[]{:S(2)}) collective-permute-start(bf16[64,1024]{1,0:T(8,128)(2,1)S(1)} %fusion.64), channel_id=1, source_target_pairs={{16,0},{17,1},{18,2},{19,3},{20,4},{21,5},{22,6},{23,7},{24,8},{25... | collective-permute-start | bytes 393224 | tf_op jit(solution)/shard_map/ppermute | solution.py:14
  96.7 1.6 copy-start.2
  98.3 1.6 copy-start.6
  99.9 11.6 %copy-start.9 = (s32[2,1,16]{2,1,0:T(1,128)S(1)}, s32[2,1,16]{2,1,0:T(1,128)}, u32[]{:S(2)}) copy-start(s32[2,1,16]{2,1,0:T(1,128)} %param.27) | copy-start | bytes 388
  106.9 13.6 %all-to-all-start = ((bf16[4,2,15360]{2,1,0:T(2,128)(2,1)}), bf16[4,2,15360]{2,1,0:T(2,128)(2,1)S(1)}, u32[]{:S(2)}, u32[]{:S(2)}) async-start(bf16[4,2,15360]{2,1,0:T(2,128)(2,1)} %reshape.131), calls=%async_computation.2 | async-start | bytes 491520 | tf_op jit(solution)/shard_map/all_to_all | solution.py:123
  135.7 22.0 %copy-start.4 = (bf16[64,1024]{1,0:T(8,128)(2,1)}, bf16[64,1024]{1,0:T(8,128)(2,1)S(1)}, u32[]{:S(2)}) copy-start(bf16[64,1024]{1,0:T(8,128)(2,1)S(1)} %fusion.70) | copy-start | bytes 393220
Sparse Core Ops, SparseCore 0:
  35.9 22.4 reduce-scatter.2
  100.0 21.1 reduce-scatter.4
